TPU v7x, 512 devices: a whole 4x8x8 slice. The times are simulated.
512 devices in a mesh: row: 32 (over z, y_hi, core), col: 16 (over y_lo, x).
Axes of the slice: x: 4, y: 8 (y_hi: 2, y_lo: 4; y = y_hi * 4 + y_lo), z: 8, core: 2. Of those that a mesh axis runs over, the one named last changes fastest.
Arguments:
- patches: bfloat16 [1024, 1024, 256], P('row', 'col'), may hold values from -6 to 6
- norm_gain: float32 [256], replicated, may hold values from 0.1 to 1.9
- w_first: bfloat16 [2, 4, 64, 64], replicated, may hold values from -0.5 to 0.5
- w_second: bfloat16 [2, 4, 64, 64], replicated, may hold values from -0.5 to 0.5
- depth_kernel: float32 [3, 3, 256], replicated, may hold values from -2 to 2
Outputs:
- mixed: bfloat16 [1024, 1024, 256], P('row', 'col')
All inputs are finite; a program needn't handle non-finite values.
Results may differ from a plain program's by a relative error of at most 0.008.
Values may be sent and summed in bfloat16 or wider, within the bound.
No kernel may reach another device: no remote copies, remote signals or barrier semaphores. Data moves between devices by JAX's collectives and lax.ppermute only.
A program may use at most 64 MiB of HBM per device.

v0:
```python
import math
import jax
import jax.numpy as jnp
from jax import lax
from jax.sharding import PartitionSpec as P


def with_halo(shard, sides, width):
    for axis, dim in sides:
        devices, length = (lax.axis_size(axis), shard.shape[dim])
        up = [(i, (i + 1) % devices) for i in range(devices)]
        down = [(j, i) for i, j in up]
        last = lax.slice_in_dim(shard, length - width, length, axis=dim)
        leading = lax.slice_in_dim(shard, 0, width, axis=dim)
        before = lax.ppermute(last, axis, up)
        after = lax.ppermute(leading, axis, down)
        shard = jnp.concatenate([before, shard, after], axis=dim)
    return shard


def phase_table(first_idx, second_idx, length):
    product = first_idx[:, None] * second_idx[None, :] % length
    phase = product.astype(jnp.float32) * (2.0 * math.pi / length)
    return (jnp.cos(phase).astype(jnp.bfloat16), jnp.sin(phase).astype(jnp.bfloat16))


def shrink(values):
    level = 0.25
    return jnp.where(
        values > level, values - level, jnp.where(values < -level, values + level, 0.0 * values)
    )


def block_product(left, weight):
    return jnp.einsum("qmbc,bcd->qmbd", left, weight, preferred_element_type=jnp.float32)


def local(patches, norm_gain, w_first, w_second, depth_kernel):
    n_row = lax.axis_size("row")
    n_col = lax.axis_size("col")
    rows_dev, cols_dev, chans = patches.shape
    patch_grid_height = rows_dev * n_row
    grid_w = cols_dev * n_col
    half = grid_w // 2
    blocks = w_first.shape[1]
    width = w_first.shape[2]
    width_factors = 1.0 / math.sqrt(grid_w)
    height_factors = 1.0 / math.sqrt(patch_grid_height)
    xf = patches.astype(jnp.float32)
    mean = jnp.mean(xf, axis=-1, keepdims=True)
    var = jnp.mean((xf - mean) ** 2, axis=-1, keepdims=True)
    normed = ((xf - mean) * lax.rsqrt(var + 1e-05) * norm_gain).astype(jnp.bfloat16)
    padded = with_halo(normed, (("row", 0), ("col", 1)), 1)
    conv = jnp.zeros((rows_dev, cols_dev, chans), jnp.float32)
    for i in range(3):
        for j in range(3):
            conv = conv + padded[i : i + rows_dev, j : j + cols_dev] * depth_kernel[i, j]
    strips = lax.all_to_all(normed, "col", split_axis=0, concat_axis=1, tiled=True)
    cos_w, sin_w = phase_table(
        jnp.arange(grid_w, dtype=jnp.int32), jnp.arange(half, dtype=jnp.int32), grid_w
    )
    forward_w = jnp.concatenate([cos_w, -sin_w], axis=1)
    spectrum_values = jnp.einsum(
        "hwc,wk->hkc", strips, forward_w, preferred_element_type=jnp.float32
    )
    spectrum_values = (spectrum_values * width_factors).astype(jnp.bfloat16)
    wre = spectrum_values[:, :half]
    wim = spectrum_values[:, half:]
    positions = jnp.arange(patch_grid_height, dtype=jnp.int32)
    across_re, across_im = (
        lax.all_to_all(wre, "col", split_axis=1, concat_axis=0, tiled=True),
        lax.all_to_all(wim, "col", split_axis=1, concat_axis=0, tiled=True),
    )
    full_re, full_im = (
        lax.all_to_all(across_re, "row", split_axis=1, concat_axis=0, tiled=True),
        lax.all_to_all(across_im, "row", split_axis=1, concat_axis=0, tiled=True),
    )
    cos_h, sin_h = phase_table(positions, positions, patch_grid_height)
    big_table = jnp.concatenate(
        [jnp.concatenate([cos_h, sin_h], axis=1), jnp.concatenate([-sin_h, cos_h], axis=1)], axis=0
    )
    stacked = jnp.concatenate([full_re, full_im], axis=0)
    spectrum = jnp.einsum("qp,pmc->qmc", big_table, stacked, preferred_element_type=jnp.float32)
    spectrum = (spectrum * height_factors).astype(jnp.bfloat16)
    modes = spectrum.shape[1]
    zre = spectrum[:patch_grid_height].reshape(patch_grid_height, modes, blocks, width)
    zim = spectrum[patch_grid_height:].reshape(patch_grid_height, modes, blocks, width)
    hre = jnp.tanh(block_product(zre, w_first[0]) - block_product(zim, w_first[1])).astype(
        jnp.bfloat16
    )
    him = jnp.tanh(block_product(zre, w_first[1]) + block_product(zim, w_first[0])).astype(
        jnp.bfloat16
    )
    spectrum_real = shrink(
        block_product(hre, w_second[0]) - block_product(him, w_second[1])
    ).astype(jnp.bfloat16)
    spectrum_imaginary = shrink(
        block_product(hre, w_second[1]) + block_product(him, w_second[0])
    ).astype(jnp.bfloat16)
    filtered = jnp.concatenate(
        [
            spectrum_real.reshape(patch_grid_height, modes, chans),
            spectrum_imaginary.reshape(patch_grid_height, modes, chans),
        ],
        axis=0,
    )
    inverse_transform = jnp.einsum(
        "qp,qmc->pmc", big_table, filtered, preferred_element_type=jnp.float32
    )
    inverse_transform = (inverse_transform * height_factors).astype(jnp.bfloat16)
    value_real = inverse_transform[:patch_grid_height]
    value_imaginary = inverse_transform[patch_grid_height:]
    part_re, part_im = (
        lax.all_to_all(value_real, "row", split_axis=0, concat_axis=1, tiled=True),
        lax.all_to_all(value_imaginary, "row", split_axis=0, concat_axis=1, tiled=True),
    )
    line_re, line_im = (
        lax.all_to_all(part_re, "col", split_axis=0, concat_axis=1, tiled=True),
        lax.all_to_all(part_im, "col", split_axis=0, concat_axis=1, tiled=True),
    )
    filter_coefficient = jnp.where(jnp.arange(half) == 0, 1.0, 2.0).astype(jnp.float32)
    inverse_w = jnp.concatenate(
        [
            (cos_w.astype(jnp.float32) * filter_coefficient).T,
            -(sin_w.astype(jnp.float32) * filter_coefficient).T,
        ],
        axis=0,
    ).astype(jnp.bfloat16)
    lines = jnp.concatenate([line_re, line_im], axis=1)
    spectral = jnp.einsum("hkc,kw->hwc", lines, inverse_w, preferred_element_type=jnp.float32)
    spectral = (spectral * width_factors).astype(jnp.bfloat16)
    home = lax.all_to_all(spectral, "col", split_axis=1, concat_axis=0, tiled=True)
    return (xf + home.astype(jnp.float32) + conv).astype(jnp.bfloat16)


def solution(mesh):
    return jax.shard_map(
        local,
        mesh=mesh,
        in_specs=(P("row", "col", None), P(), P(), P(), P()),
        out_specs=P("row", "col", None),
        check_vma=False,
    )
```

profile of v0, /device:TPU:63, one launch (start us, length us, event | category | flops | bytes accessed | tf_op | source)
XLA Modules:
  0.0 328.7 jit_solution(4939369207946088311)
XLA Ops:
  0.0 1.7 convert_reduce_fusion
  1.7 1.9 fusion.10
  3.6 1.5 fusion.12
  5.1 6.9 %all-to-all-start = ((bf16[32,64,256]{2,1,0:T(8,128)(2,1)}), bf16[32,64,256]{2,1,0:T(8,128)(2,1)S(1)}, u32[]{:S(2)}, u32[]{:S(2)}) async-start(bf16[32,64,256]{2,1,0:T(8,128)(2,1)} %fusion.12), calls=%async_computation | async-start | bytes 2097152 | tf_op jit(solution)/shard_map/all_to_all | solution.py:58
  12.1 7.8 %cosine_convert_fusion.1 = bf16[1024,512]{0,1:T(8,128)(2,1)S(1)} fusion(), kind=kLoop, calls=%fused_computation.50 | loop fusion | flops 7864320 | bytes 1048576 | tf_op jit(solution)/shard_map/convert_element_type | solution.py:24
  19.8 8.6 %fusion.41 = bf16[1024,512]{0,1:T(8,128)(2,1)} fusion(), kind=kLoop, calls=%fused_computation.75 | loop fusion | flops 9437184 | bytes 1048576 | tf_op jit(solution)/shard_map/neg | solution.py:62
  28.4 6.1 %all-to-all-done = bf16[32,64,256]{2,1,0:T(8,128)(2,1)S(1)} async-done(((bf16[32,64,256]{2,1,0:T(8,128)(2,1)}), bf16[32,64,256]{2,1,0:T(8,128)(2,1)S(1)}, u32[]{:S(2)}, u32[]{:S(2)}) %all-to-all-start) | async-done | bytes 1048608 | tf_op jit(solution)/shard_map/all_to_all | solution.py:58
  34.6 1.1 copy-done.3
  35.7 1.3 fusion.33
  37.1 1.3 copy.51
  38.4 7.4 %all-to-all-start.1 = ((bf16[2,512,256]{2,0,1:T(2,128)(2,1)}), bf16[2,512,256]{2,0,1:T(2,128)(2,1)S(1)}, u32[]{:S(2)}, u32[]{:S(2)}) async-start(bf16[2,512,256]{2,0,1:T(2,128)(2,1)} %copy.51), calls=%async_computation.1 | async-start | bytes 1048576 | tf_op jit(solution)/shard_map/all_to_all | solution.py:71
  45.8 1.3 copy.55
  47.1 10.5 %all-to-all-done.1 = bf16[2,512,256]{2,0,1:T(2,128)(2,1)S(1)} async-done(((bf16[2,512,256]{2,0,1:T(2,128)(2,1)}), bf16[2,512,256]{2,0,1:T(2,128)(2,1)S(1)}, u32[]{:S(2)}, u32[]{:S(2)}) %all-to-all-start.1) | async-done | bytes 524320 | tf_op jit(solution)/shard_map/all_to_all | solution.py:71
  57.7 6.7 %all-to-all-start.3 = ((bf16[2,512,256]{2,0,1:T(2,128)(2,1)}), bf16[2,512,256]{2,0,1:T(2,128)(2,1)S(1)}, u32[]{:S(2)}, u32[]{:S(2)}) async-start(bf16[2,512,256]{2,0,1:T(2,128)(2,1)} %copy.55), calls=%async_computation.3 | async-start | bytes 1048576 | tf_op jit(solution)/shard_map/all_to_all | solution.py:72
  64.5 1.1 copy.54
  65.5 10.0 %all-to-all-done.3 = bf16[2,512,256]{2,0,1:T(2,128)(2,1)S(1)} async-done(((bf16[2,512,256]{2,0,1:T(2,128)(2,1)}), bf16[2,512,256]{2,0,1:T(2,128)(2,1)S(1)}, u32[]{:S(2)}, u32[]{:S(2)}) %all-to-all-start.3) | async-done | bytes 524320 | tf_op jit(solution)/shard_map/all_to_all | solution.py:72
  75.5 17.7 %all-to-all-start.2 = ((bf16[32,32,256]{2,0,1:T(8,128)(2,1)}), bf16[32,32,256]{2,0,1:T(8,128)(2,1)S(1)}, u32[]{:S(2)}, u32[]{:S(2)}) async-start(bf16[32,32,256]{2,0,1:T(8,128)(2,1)} %copy.54), calls=%async_computation.2 | async-start | bytes 1048576 | tf_op jit(solution)/shard_map/all_to_all | solution.py:75
  93.3 1.1 copy.58
  94.4 16.0 %all-to-all-done.2 = bf16[32,32,256]{2,0,1:T(8,128)(2,1)S(1)} async-done(((bf16[32,32,256]{2,0,1:T(8,128)(2,1)}), bf16[32,32,256]{2,0,1:T(8,128)(2,1)S(1)}, u32[]{:S(2)}, u32[]{:S(2)}) %all-to-all-start.2) | async-done | bytes 524320 | tf_op jit(solution)/shard_map/all_to_all | solution.py:75
  111.2 8.0 %all-to-all-start.4 = ((bf16[32,32,256]{2,0,1:T(8,128)(2,1)}), bf16[32,32,256]{2,0,1:T(8,128)(2,1)}, u32[]{:S(2)}, u32[]{:S(2)}) async-start(bf16[32,32,256]{2,0,1:T(8,128)(2,1)} %copy.58), calls=%async_computation.4 | async-start | bytes 1048576 | tf_op jit(solution)/shard_map/all_to_all | solution.py:76
  119.2 15.8 %fusion.49 = bf16[1024,1024]{1,0:T(8,128)(2,1)S(1)} fusion(), kind=kLoop, calls=%fused_computation.89 | loop fusion | flops 18874368 | bytes 2097152 | tf_op jit(solution)/shard_map/neg | solution.py:80
  135.1 17.7 %sine_convert_fusion = (bf16[1024,1024]{1,0:T(8,128)(2,1)}, bf16[1024,1024]{1,0:T(8,128)(2,1)}) fusion(), kind=kLoop, calls=%fused_computation.7 | loop fusion | flops 16777216 | bytes 4194304 | tf_op jit(solution)/shard_map/convert_element_type | solution.py:24
  152.8 14.9 %fusion.6 = bf16[2048,256]{0,1:T(8,128)(2,1)S(1)} fusion(bf16[1024,1024]{1,0:T(8,128)(2,1)} %get-tuple-element.29, bf16[1024,1024]{1,0:T(8,128)(2,1)S(1)} %fusion.49, bf16[1024,1024]{1,0:T(8,128)(2,1)} %get-tuple-element.28, bf16[1024,1,256]{2,0,1:T(8,128)(2,1)} %bitcast.17, bf16[1024,1,256]{2,0,1:T(8,128)(2,1)} %bitcast.166), kind=kOutput, calls=%fused_computation.23 | convolution fusion | flops 2184183808 | bytes 8388608 | tf_op jit(solution)/shard_map/qp,pmc->qmc/dot_general | solution.py:83
  173.1 2.4 fusion.7
  178.2 12.2 %all-to-all-start.5 = ((bf16[32,2,4096]{2,1,0:T(2,128)(2,1)}), bf16[32,2,4096]{2,1,0:T(2,128)(2,1)S(1)}, u32[]{:S(2)}, u32[]{:S(2)}) async-start(bf16[32,2,4096]{2,1,0:T(2,128)(2,1)} %reshape.124), calls=%async_computation.5 | async-start | bytes 1048576 | tf_op jit(solution)/shard_map/all_to_all | solution.py:114
  192.6 14.9 %all-to-all-done.5 = bf16[32,2,4096]{2,1,0:T(2,128)(2,1)S(1)} async-done(((bf16[32,2,4096]{2,1,0:T(2,128)(2,1)}), bf16[32,2,4096]{2,1,0:T(2,128)(2,1)S(1)}, u32[]{:S(2)}, u32[]{:S(2)}) %all-to-all-start.5) | async-done | bytes 524320 | tf_op jit(solution)/shard_map/all_to_all | solution.py:114
  207.5 8.0 %all-to-all-start.7 = ((bf16[32,2,4096]{2,1,0:T(2,128)(2,1)}), bf16[32,2,4096]{2,1,0:T(2,128)(2,1)S(1)}, u32[]{:S(2)}, u32[]{:S(2)}) async-start(bf16[32,2,4096]{2,1,0:T(2,128)(2,1)} %reshape.122), calls=%async_computation.7 | async-start | bytes 1048576 | tf_op jit(solution)/shard_map/all_to_all | solution.py:115
  216.1 1.1 copy.65
  217.3 15.3 %all-to-all-done.7 = bf16[32,2,4096]{2,1,0:T(2,128)(2,1)S(1)} async-done(((bf16[32,2,4096]{2,1,0:T(2,128)(2,1)}), bf16[32,2,4096]{2,1,0:T(2,128)(2,1)S(1)}, u32[]{:S(2)}, u32[]{:S(2)}) %all-to-all-start.7) | async-done | bytes 524320 | tf_op jit(solution)/shard_map/all_to_all | solution.py:115
  232.6 7.9 %all-to-all-start.6 = ((bf16[32,32,256]{2,1,0:T(8,128)(2,1)}), bf16[32,32,256]{2,1,0:T(8,128)(2,1)S(1)}, u32[]{:S(2)}, u32[]{:S(2)}) async-start(bf16[32,32,256]{2,1,0:T(8,128)(2,1)} %copy.65), calls=%async_computation.6 | async-start | bytes 1048576 | tf_op jit(solution)/shard_map/all_to_all | solution.py:118
  241.2 1.1 copy.68
  242.2 10.2 %all-to-all-done.6 = bf16[32,32,256]{2,1,0:T(8,128)(2,1)S(1)} async-done(((bf16[32,32,256]{2,1,0:T(8,128)(2,1)}), bf16[32,32,256]{2,1,0:T(8,128)(2,1)S(1)}, u32[]{:S(2)}, u32[]{:S(2)}) %all-to-all-start.6) | async-done | bytes 524320 | tf_op jit(solution)/shard_map/all_to_all | solution.py:118
  252.4 6.9 %all-to-all-start.8 = ((bf16[32,32,256]{2,1,0:T(8,128)(2,1)}), bf16[32,32,256]{2,1,0:T(8,128)(2,1)S(1)}, u32[]{:S(2)}, u32[]{:S(2)}) async-start(bf16[32,32,256]{2,1,0:T(8,128)(2,1)} %copy.68), calls=%async_computation.8 | async-start | bytes 1048576 | tf_op jit(solution)/shard_map/all_to_all | solution.py:119
  259.3 9.4 %multiply_convert_fusion.2 = (bf16[512,1024]{0,1:T(8,128)(2,1)S(1)}, bf16[512,1024]{0,1:T(8,128)(2,1)}) fusion(f32[512]{0:T(512)S(1)} %fusion.70), kind=kLoop, calls=%fused_computation.55 | loop fusion | flops 12058624 | bytes 2099200 | tf_op jit(solution)/shard_map/convert.7
  269.6 1.4 all-to-all-done.8
  271.1 2.6 fusion.34
  273.7 2.0 copy.70
  275.7 6.8 %all-to-all-start.9 = ((bf16[2,1024,256]{2,0,1:T(2,128)(2,1)}), bf16[2,1024,256]{2,0,1:T(2,128)(2,1)}, u32[]{:S(2)}, u32[]{:S(2)}) async-start(bf16[2,1024,256]{2,0,1:T(2,128)(2,1)} %copy.70), calls=%async_computation.9 | async-start | bytes 2097152 | tf_op jit(solution)/shard_map/all_to_all | solution.py:132
  283.3 8.8 %collective-permute-start = (bf16[1,64,256]{2,1,0:T(8,128)(2,1)S(1)}, bf16[1,64,256]{2,1,0:T(8,128)(2,1)S(1)}, u32[]{:S(2)}, u32[]{:S(2)}) collective-permute-start(bf16[1,64,256]{2,1,0:T(8,128)(2,1)S(1)} %get-tuple-element.9), channel_id=1, source_target_pairs={{0,16},{16,32},{32,48},{48,64},{64,80},{80,96},{96,112},{112,128},... | collective-permute-start | bytes 98312 | tf_op jit(solution)/shard_map/ppermute | solution.py:15
  292.2 1.9 collective-permute-start.1
  294.1 4.3 %collective-permute-done = bf16[1,64,256]{2,1,0:T(8,128)(2,1)S(1)} collective-permute-done((bf16[1,64,256]{2,1,0:T(8,128)(2,1)S(1)}, bf16[1,64,256]{2,1,0:T(8,128)(2,1)S(1)}, u32[]{:S(2)}, u32[]{:S(2)}) %collective-permute-start) | collective-permute-done | bytes 32800 | tf_op jit(solution)/shard_map/ppermute | solution.py:15
  298.4 8.2 %collective-permute-done.1 = bf16[1,64,256]{2,1,0:T(8,128)(2,1)S(1)} collective-permute-done((bf16[1,64,256]{2,1,0:T(8,128)(2,1)S(1)}, bf16[1,64,256]{2,1,0:T(8,128)(2,1)S(1)}, u32[]{:S(2)}, u32[]{:S(2)}) %collective-permute-start.1) | collective-permute-done | bytes 32800 | tf_op jit(solution)/shard_map/ppermute | solution.py:16
  307.6 1.9 collective-permute-start.2
  309.6 3.6 %collective-permute-start.3 = (bf16[34,1,256]{2,1,0:T(2,128)(2,1)S(1)}, bf16[34,1,256]{2,1,0:T(2,128)(2,1)S(1)}, u32[]{:S(2)}, u32[]{:S(2)}) collective-permute-start(bf16[34,1,256]{2,1,0:T(2,128)(2,1)S(1)} %get-tuple-element.8), channel_id=1, source_target_pairs={{1,0},{2,1},{3,2},{4,3},{5,4},{6,5},{7,6},{8,7},{9,8},{10,9},{11,1... | collective-permute-start | bytes 52232 | tf_op jit(solution)/shard_map/ppermute | solution.py:16
  313.8 4.3 %collective-permute-done.3 = bf16[34,1,256]{2,1,0:T(2,128)(2,1)S(1)} collective-permute-done((bf16[34,1,256]{2,1,0:T(2,128)(2,1)S(1)}, bf16[34,1,256]{2,1,0:T(2,128)(2,1)S(1)}, u32[]{:S(2)}, u32[]{:S(2)}) %collective-permute-start.3) | collective-permute-done | bytes 17440 | tf_op jit(solution)/shard_map/ppermute | solution.py:16
  318.2 2.3 maximum_maximum_fusion.3
  320.5 2.1 convert_bitcast_fusion
  323.4 5.2 %fusion.14 = bf16[32,64,256]{2,1,0:T(8,128)(2,1)} fusion(bf16[32,64,256]{2,1,0:T(8,128)(2,1)S(1)} %copy-done, f32[16,2,64,256]{3,2,1,0:T(8,128)S(1)} %copy.71, bf16[32,64,256]{2,1,0:T(8,128)(2,1)} %fusion.12, bf16[34,65,256]{2,1,0:T(8,128)(2,1)S(1)} %get-tuple-element.6, bf16[1,64,256]{2,1,0:T(8,128)(2,1)S(1)} %copy-done.9, ...), kind=kLoop, calls=%fused_computation.31 | loop fusion | flops 16777216 | bytes 11609088 | tf_op jit(solution)/shard_map/convert_element_type | solution.py:133
  (82 shorter events, 16.7 us)
Async XLA Ops:
  0.0 3.6 %copy-start = (bf16[32,64,256]{2,1,0:T(8,128)(2,1)S(1)}, bf16[32,64,256]{2,1,0:T(8,128)(2,1)}, u32[]{:S(2)}) copy-start(bf16[32,64,256]{2,1,0:T(8,128)(2,1)} %param.5) | copy-start | bytes 3145732
  0.0 3.6 %copy-start.21 = (f32[256]{0:T(256)S(1)}, f32[256]{0:T(256)}, u32[]{:S(2)}) copy-start(f32[256]{0:T(256)} %param.6) | copy-start | bytes 3076
  5.1 29.4 %all-to-all-start = ((bf16[32,64,256]{2,1,0:T(8,128)(2,1)}), bf16[32,64,256]{2,1,0:T(8,128)(2,1)S(1)}, u32[]{:S(2)}, u32[]{:S(2)}) async-start(bf16[32,64,256]{2,1,0:T(8,128)(2,1)} %fusion.12), calls=%async_computation | async-start | bytes 2097152 | tf_op jit(solution)/shard_map/all_to_all | solution.py:58
  34.5 1.2 copy-start.3
  38.4 19.3 %all-to-all-start.1 = ((bf16[2,512,256]{2,0,1:T(2,128)(2,1)}), bf16[2,512,256]{2,0,1:T(2,128)(2,1)S(1)}, u32[]{:S(2)}, u32[]{:S(2)}) async-start(bf16[2,512,256]{2,0,1:T(2,128)(2,1)} %copy.51), calls=%async_computation.1 | async-start | bytes 1048576 | tf_op jit(solution)/shard_map/all_to_all | solution.py:71
  57.7 17.8 %all-to-all-start.3 = ((bf16[2,512,256]{2,0,1:T(2,128)(2,1)}), bf16[2,512,256]{2,0,1:T(2,128)(2,1)S(1)}, u32[]{:S(2)}, u32[]{:S(2)}) async-start(bf16[2,512,256]{2,0,1:T(2,128)(2,1)} %copy.55), calls=%async_computation.3 | async-start | bytes 1048576 | tf_op jit(solution)/shard_map/all_to_all | solution.py:72
  75.5 34.8 %all-to-all-start.2 = ((bf16[32,32,256]{2,0,1:T(8,128)(2,1)}), bf16[32,32,256]{2,0,1:T(8,128)(2,1)S(1)}, u32[]{:S(2)}, u32[]{:S(2)}) async-start(bf16[32,32,256]{2,0,1:T(8,128)(2,1)} %copy.54), calls=%async_computation.2 | async-start | bytes 1048576 | tf_op jit(solution)/shard_map/all_to_all | solution.py:75
  110.3 0.8 copy-start.5
  111.2 41.6 %all-to-all-start.4 = ((bf16[32,32,256]{2,0,1:T(8,128)(2,1)}), bf16[32,32,256]{2,0,1:T(8,128)(2,1)}, u32[]{:S(2)}, u32[]{:S(2)}) async-start(bf16[32,32,256]{2,0,1:T(8,128)(2,1)} %copy.58), calls=%async_computation.4 | async-start | bytes 1048576 | tf_op jit(solution)/shard_map/all_to_all | solution.py:76
  167.6 0.9 copy-start.4
  168.9 0.9 copy-start.10
  170.8 1.6 copy-start.1
  170.9 2.2 copy-start.2
  178.2 29.3 %all-to-all-start.5 = ((bf16[32,2,4096]{2,1,0:T(2,128)(2,1)}), bf16[32,2,4096]{2,1,0:T(2,128)(2,1)S(1)}, u32[]{:S(2)}, u32[]{:S(2)}) async-start(bf16[32,2,4096]{2,1,0:T(2,128)(2,1)} %reshape.124), calls=%async_computation.5 | async-start | bytes 1048576 | tf_op jit(solution)/shard_map/all_to_all | solution.py:114
  207.5 25.1 %all-to-all-start.7 = ((bf16[32,2,4096]{2,1,0:T(2,128)(2,1)}), bf16[32,2,4096]{2,1,0:T(2,128)(2,1)S(1)}, u32[]{:S(2)}, u32[]{:S(2)}) async-start(bf16[32,2,4096]{2,1,0:T(2,128)(2,1)} %reshape.122), calls=%async_computation.7 | async-start | bytes 1048576 | tf_op jit(solution)/shard_map/all_to_all | solution.py:115
  232.6 19.8 %all-to-all-start.6 = ((bf16[32,32,256]{2,1,0:T(8,128)(2,1)}), bf16[32,32,256]{2,1,0:T(8,128)(2,1)S(1)}, u32[]{:S(2)}, u32[]{:S(2)}) async-start(bf16[32,32,256]{2,1,0:T(8,128)(2,1)} %copy.65), calls=%async_computation.6 | async-start | bytes 1048576 | tf_op jit(solution)/shard_map/all_to_all | solution.py:118
  252.4 18.6 %all-to-all-start.8 = ((bf16[32,32,256]{2,1,0:T(8,128)(2,1)}), bf16[32,32,256]{2,1,0:T(8,128)(2,1)S(1)}, u32[]{:S(2)}, u32[]{:S(2)}) async-start(bf16[32,32,256]{2,1,0:T(8,128)(2,1)} %copy.68), calls=%async_computation.8 | async-start | bytes 1048576 | tf_op jit(solution)/shard_map/all_to_all | solution.py:119
  275.7 37.5 %copy-start.11 = (f32[3,3,256]{2,1,0:T(4,128)S(1)}, f32[3,3,256]{2,1,0:T(4,128)}, u32[]{:S(2)}) copy-start(f32[3,3,256]{2,1,0:T(4,128)} %param.9) | copy-start | bytes 27652
  275.7 44.7 %all-to-all-start.9 = ((bf16[2,1024,256]{2,0,1:T(2,128)(2,1)}), bf16[2,1024,256]{2,0,1:T(2,128)(2,1)}, u32[]{:S(2)}, u32[]{:S(2)}) async-start(bf16[2,1024,256]{2,0,1:T(2,128)(2,1)} %copy.70), calls=%async_computation.9 | async-start | bytes 2097152 | tf_op jit(solution)/shard_map/all_to_all | solution.py:132
  283.3 15.0 %collective-permute-start = (bf16[1,64,256]{2,1,0:T(8,128)(2,1)S(1)}, bf16[1,64,256]{2,1,0:T(8,128)(2,1)S(1)}, u32[]{:S(2)}, u32[]{:S(2)}) collective-permute-start(bf16[1,64,256]{2,1,0:T(8,128)(2,1)S(1)} %get-tuple-element.9), channel_id=1, source_target_pairs={{0,16},{16,32},{32,48},{48,64},{64,80},{80,96},{96,112},{112,128},... | collective-permute-start | bytes 98312 | tf_op jit(solution)/shard_map/ppermute | solution.py:15
  292.2 14.4 %collective-permute-start.1 = (bf16[1,64,256]{2,1,0:T(8,128)(2,1)S(1)}, bf16[1,64,256]{2,1,0:T(8,128)(2,1)S(1)}, u32[]{:S(2)}, u32[]{:S(2)}) collective-permute-start(bf16[1,64,256]{2,1,0:T(8,128)(2,1)S(1)} %get-tuple-element.10), channel_id=1, source_target_pairs={{16,0},{32,16},{48,32},{64,48},{80,64},{96,80},{112,96},{128,112},... | collective-permute-start | bytes 98312 | tf_op jit(solution)/shard_map/ppermute | solution.py:16
  298.4 19.8 %copy-start.6 = (bf16[1,64,256]{2,1,0:T(8,128)(2,1)}, bf16[1,64,256]{2,1,0:T(8,128)(2,1)S(1)}, u32[]{:S(2)}) copy-start(bf16[1,64,256]{2,1,0:T(8,128)(2,1)S(1)} %collective-permute-done) | copy-start | bytes 98308
  306.6 11.6 %copy-start.8 = (bf16[1,64,256]{2,1,0:T(8,128)(2,1)}, bf16[1,64,256]{2,1,0:T(8,128)(2,1)S(1)}, u32[]{:S(2)}) copy-start(bf16[1,64,256]{2,1,0:T(8,128)(2,1)S(1)} %collective-permute-done.1) | copy-start | bytes 98308
  307.6 6.2 %collective-permute-start.2 = (bf16[34,1,256]{2,1,0:T(2,128)(2,1)S(1)}, bf16[34,1,256]{2,1,0:T(2,128)(2,1)S(1)}, u32[]{:S(2)}, u32[]{:S(2)}) collective-permute-start(bf16[34,1,256]{2,1,0:T(2,128)(2,1)S(1)} %get-tuple-element.7), channel_id=1, source_target_pairs={{0,1},{1,2},{2,3},{3,4},{4,5},{5,6},{6,7},{7,8},{8,9},{9,10},{10,1... | collective-permute-start | bytes 52232 | tf_op jit(solution)/shard_map/ppermute | solution.py:15
  309.6 8.6 %collective-permute-start.3 = (bf16[34,1,256]{2,1,0:T(2,128)(2,1)S(1)}, bf16[34,1,256]{2,1,0:T(2,128)(2,1)S(1)}, u32[]{:S(2)}, u32[]{:S(2)}) collective-permute-start(bf16[34,1,256]{2,1,0:T(2,128)(2,1)S(1)} %get-tuple-element.8), channel_id=1, source_target_pairs={{1,0},{2,1},{3,2},{4,3},{5,4},{6,5},{7,6},{8,7},{9,8},{10,9},{11,1... | collective-permute-start | bytes 52232 | tf_op jit(solution)/shard_map/ppermute | solution.py:16
  322.6 0.8 copy-start.7
  322.6 0.8 copy-start.9
  322.6 0.8 copy-start.12
  322.6 0.8 copy-start.13
  322.6 0.7 copy-start.14
  322.7 0.7 copy-start.15
  322.7 0.7 copy-start.16
  322.7 0.7 copy-start.17
  322.7 0.7 copy-start.18
  322.7 0.7 copy-start.19
  322.7 0.7 copy-start.20
where the time goes:
time: 330 us; the launch traced here: 329 us
  starting transfers between devices  105 us (32%)
  waiting for transfers between devices  101 us (31%)
  other arithmetic  77.1 us (23%)
  matrix products  24.2 us (7%)
  local copies, waits for them, and re-layouts  20.7 us (6%)
    convert_element_type x1, other arithmetic, phase_table(): jnp.sin(phase).astype(jnp.bfloat16)  17.7 us
    all_to_all x1, starting transfers between devices, local(): lax.all_to_all(across_re, 'row', split_axis=1, concat_axis=0, tiled=True)  17.7 us
    all_to_all x1, waiting for transfers between devices, local(): lax.all_to_all(across_re, 'row', split_axis=1, concat_axis=0, tiled=True)  16 us
    neg x1, other arithmetic, local(): -sin_h  15.8 us
    all_to_all x1, waiting for transfers between devices, local(): lax.all_to_all(value_imaginary, 'row', split_axis=0, concat_axis=1, tiled...  15.3 us
    all_to_all x1, waiting for transfers between devices, local(): lax.all_to_all(value_real, 'row', split_axis=0, concat_axis=1, tiled=True)  14.9 us
    dot_general x1, matrix products, local(): jnp.einsum('qp,pmc->qmc', big_table, stacked, preferred_element_type=jnp....  14.9 us
    ppermute x2, waiting for transfers between devices, with_halo(): after = lax.ppermute(leading, axis, down)  12.5 us
  transfers between devices with their start and end apart: 14, of which 11 were waited for; matrix products, arithmetic and copies ran while one was open for 23% of the time, Pallas kernels for 0%

commit v1 on v0

--- a/solution.py
+++ b/solution.py
@@ -115,7 +115,12 @@
         lax.all_to_all(value_imaginary, "row", split_axis=0, concat_axis=1, tiled=True),
     )
     line_re, line_im = (
-        lax.all_to_all(part_re, "col", split_axis=0, concat_axis=1, tiled=True),
+        jnp.concatenate(
+            lax.all_to_all(
+                jnp.stack(jnp.split(part_re, lax.axis_size("col"), axis=0)), "col", 0, 0
+            ),
+            axis=1,
+        ),
         lax.all_to_all(part_im, "col", split_axis=0, concat_axis=1, tiled=True),
     )
     filter_coefficient = jnp.where(jnp.arange(half) == 0, 1.0, 2.0).astype(jnp.float32)

time: 330 us -> 330 us (level)
  local copies, waits for them, and re-layouts: 20.7 us -> 29.8 us
  waiting for transfers between devices: 101 us -> 92.2 us
    unnamed x52 -> x67, local copies, waits for them, and re-layouts: 8.08 us -> 17.6 us
    all_to_all x1, waiting for transfers between devices: 15.3 us -> 6.29 us  [local(): lax.all_to_all(value_imaginary, 'row', split_axis=0, concat_axis=1, tiled...]
  transfers between devices with their start and end apart: 14 -> 14, of which waited for: 11 -> 11; matrix products, arithmetic and copies ran while one was open for 23% -> 25% of each run, Pallas kernels for 0% -> 0%
where the time goes in v1:
time: 330 us; the launch traced here: 329 us
  starting transfers between devices  105 us (32%)
  waiting for transfers between devices  92.2 us (28%)
  other arithmetic  77.1 us (23%)
  local copies, waits for them, and re-layouts  29.8 us (9%)
  matrix products  24.2 us (7%)
    convert_element_type x1, other arithmetic, phase_table(): jnp.sin(phase).astype(jnp.bfloat16)  17.7 us
    all_to_all x1, starting transfers between devices, local(): lax.all_to_all(across_re, 'row', split_axis=1, concat_axis=0, tiled=True)  17.7 us
    unnamed x67, local copies, waits for them, and re-layouts  17.6 us
    all_to_all x1, waiting for transfers between devices, local(): lax.all_to_all(across_re, 'row', split_axis=1, concat_axis=0, tiled=True)  16 us
    neg x1, other arithmetic, local(): -sin_h  15.8 us
    all_to_all x1, waiting for transfers between devices, local(): lax.all_to_all(value_real, 'row', split_axis=0, concat_axis=1, tiled=True)  14.9 us
    dot_general x1, matrix products, local(): jnp.einsum('qp,pmc->qmc', big_table, stacked, preferred_element_type=jnp....  14.9 us
    ppermute x2, waiting for transfers between devices, with_halo(): after = lax.ppermute(leading, axis, down)  12.8 us
  transfers between devices with their start and end apart: 14, of which 11 were waited for; matrix products, arithmetic and copies ran while one was open for 25% of the time, Pallas kernels for 0%

profile of v1, /device:TPU:63, one launch (start us, length us, event | category | flops | bytes accessed | tf_op | source)
XLA Modules:
  0.0 328.7 jit_solution(14973742373270852814)
XLA Ops:
  0.0 1.7 convert_reduce_fusion
  1.7 1.9 fusion.10
  3.6 1.5 fusion.12
  5.1 6.9 %all-to-all-start = ((bf16[32,64,256]{2,1,0:T(8,128)(2,1)}), bf16[32,64,256]{2,1,0:T(8,128)(2,1)S(1)}, u32[]{:S(2)}, u32[]{:S(2)}) async-start(bf16[32,64,256]{2,1,0:T(8,128)(2,1)} %fusion.12), calls=%async_computation | async-start | bytes 2097152 | tf_op jit(solution)/shard_map/all_to_all | solution.py:58
  12.1 7.8 %cosine_convert_fusion.1 = bf16[1024,512]{0,1:T(8,128)(2,1)S(1)} fusion(), kind=kLoop, calls=%fused_computation.50 | loop fusion | flops 7864320 | bytes 1048576 | tf_op jit(solution)/shard_map/convert_element_type | solution.py:24
  19.8 8.6 %fusion.41 = bf16[1024,512]{0,1:T(8,128)(2,1)} fusion(), kind=kLoop, calls=%fused_computation.75 | loop fusion | flops 9437184 | bytes 1048576 | tf_op jit(solution)/shard_map/neg | solution.py:62
  28.4 6.1 %all-to-all-done = bf16[32,64,256]{2,1,0:T(8,128)(2,1)S(1)} async-done(((bf16[32,64,256]{2,1,0:T(8,128)(2,1)}), bf16[32,64,256]{2,1,0:T(8,128)(2,1)S(1)}, u32[]{:S(2)}, u32[]{:S(2)}) %all-to-all-start) | async-done | bytes 1048608 | tf_op jit(solution)/shard_map/all_to_all | solution.py:58
  34.6 1.1 copy-done.3
  35.7 1.3 fusion.33
  37.1 1.3 copy.49
  38.4 7.4 %all-to-all-start.1 = ((bf16[2,512,256]{2,0,1:T(2,128)(2,1)}), bf16[2,512,256]{2,0,1:T(2,128)(2,1)S(1)}, u32[]{:S(2)}, u32[]{:S(2)}) async-start(bf16[2,512,256]{2,0,1:T(2,128)(2,1)} %copy.49), calls=%async_computation.1 | async-start | bytes 1048576 | tf_op jit(solution)/shard_map/all_to_all | solution.py:71
  45.8 1.3 copy.53
  47.1 10.5 %all-to-all-done.1 = bf16[2,512,256]{2,0,1:T(2,128)(2,1)S(1)} async-done(((bf16[2,512,256]{2,0,1:T(2,128)(2,1)}), bf16[2,512,256]{2,0,1:T(2,128)(2,1)S(1)}, u32[]{:S(2)}, u32[]{:S(2)}) %all-to-all-start.1) | async-done | bytes 524320 | tf_op jit(solution)/shard_map/all_to_all | solution.py:71
  57.7 6.7 %all-to-all-start.3 = ((bf16[2,512,256]{2,0,1:T(2,128)(2,1)}), bf16[2,512,256]{2,0,1:T(2,128)(2,1)S(1)}, u32[]{:S(2)}, u32[]{:S(2)}) async-start(bf16[2,512,256]{2,0,1:T(2,128)(2,1)} %copy.53), calls=%async_computation.3 | async-start | bytes 1048576 | tf_op jit(solution)/shard_map/all_to_all | solution.py:72
  64.5 1.1 copy.52
  65.5 10.0 %all-to-all-done.3 = bf16[2,512,256]{2,0,1:T(2,128)(2,1)S(1)} async-done(((bf16[2,512,256]{2,0,1:T(2,128)(2,1)}), bf16[2,512,256]{2,0,1:T(2,128)(2,1)S(1)}, u32[]{:S(2)}, u32[]{:S(2)}) %all-to-all-start.3) | async-done | bytes 524320 | tf_op jit(solution)/shard_map/all_to_all | solution.py:72
  75.5 17.7 %all-to-all-start.2 = ((bf16[32,32,256]{2,0,1:T(8,128)(2,1)}), bf16[32,32,256]{2,0,1:T(8,128)(2,1)S(1)}, u32[]{:S(2)}, u32[]{:S(2)}) async-start(bf16[32,32,256]{2,0,1:T(8,128)(2,1)} %copy.52), calls=%async_computation.2 | async-start | bytes 1048576 | tf_op jit(solution)/shard_map/all_to_all | solution.py:75
  93.3 1.1 copy.56
  94.4 16.0 %all-to-all-done.2 = bf16[32,32,256]{2,0,1:T(8,128)(2,1)S(1)} async-done(((bf16[32,32,256]{2,0,1:T(8,128)(2,1)}), bf16[32,32,256]{2,0,1:T(8,128)(2,1)S(1)}, u32[]{:S(2)}, u32[]{:S(2)}) %all-to-all-start.2) | async-done | bytes 524320 | tf_op jit(solution)/shard_map/all_to_all | solution.py:75
  111.2 8.0 %all-to-all-start.4 = ((bf16[32,32,256]{2,0,1:T(8,128)(2,1)}), bf16[32,32,256]{2,0,1:T(8,128)(2,1)}, u32[]{:S(2)}, u32[]{:S(2)}) async-start(bf16[32,32,256]{2,0,1:T(8,128)(2,1)} %copy.56), calls=%async_computation.4 | async-start | bytes 1048576 | tf_op jit(solution)/shard_map/all_to_all | solution.py:76
  119.2 15.8 %fusion.49 = bf16[1024,1024]{1,0:T(8,128)(2,1)S(1)} fusion(), kind=kLoop, calls=%fused_computation.89 | loop fusion | flops 18874368 | bytes 2097152 | tf_op jit(solution)/shard_map/neg | solution.py:80
  135.1 17.7 %sine_convert_fusion = (bf16[1024,1024]{1,0:T(8,128)(2,1)}, bf16[1024,1024]{1,0:T(8,128)(2,1)}) fusion(), kind=kLoop, calls=%fused_computation.7 | loop fusion | flops 16777216 | bytes 4194304 | tf_op jit(solution)/shard_map/convert_element_type | solution.py:24
  152.8 14.9 %fusion.6 = bf16[2048,256]{0,1:T(8,128)(2,1)S(1)} fusion(bf16[1024,1024]{1,0:T(8,128)(2,1)} %get-tuple-element.29, bf16[1024,1024]{1,0:T(8,128)(2,1)S(1)} %fusion.49, bf16[1024,1024]{1,0:T(8,128)(2,1)} %get-tuple-element.28, bf16[1024,1,256]{2,0,1:T(8,128)(2,1)} %bitcast.17, bf16[1024,1,256]{2,0,1:T(8,128)(2,1)} %bitcast.241), kind=kOutput, calls=%fused_computation.23 | convolution fusion | flops 2184183808 | bytes 8388608 | tf_op jit(solution)/shard_map/qp,pmc->qmc/dot_general | solution.py:83
  173.1 2.4 fusion.7
  178.2 12.2 %all-to-all-start.5 = ((bf16[32,2,4096]{2,1,0:T(2,128)(2,1)}), bf16[32,2,4096]{2,1,0:T(2,128)(2,1)S(1)}, u32[]{:S(2)}, u32[]{:S(2)}) async-start(bf16[32,2,4096]{2,1,0:T(2,128)(2,1)} %reshape.164), calls=%async_computation.5 | async-start | bytes 1048576 | tf_op jit(solution)/shard_map/all_to_all | solution.py:114
  192.6 14.9 %all-to-all-done.5 = bf16[32,2,4096]{2,1,0:T(2,128)(2,1)S(1)} async-done(((bf16[32,2,4096]{2,1,0:T(2,128)(2,1)}), bf16[32,2,4096]{2,1,0:T(2,128)(2,1)S(1)}, u32[]{:S(2)}, u32[]{:S(2)}) %all-to-all-start.5) | async-done | bytes 524320 | tf_op jit(solution)/shard_map/all_to_all | solution.py:114
  207.5 8.0 %all-to-all-start.7 = ((bf16[32,2,4096]{2,1,0:T(2,128)(2,1)}), bf16[32,2,4096]{2,1,0:T(2,128)(2,1)S(1)}, u32[]{:S(2)}, u32[]{:S(2)}) async-start(bf16[32,2,4096]{2,1,0:T(2,128)(2,1)} %reshape.162), calls=%async_computation.7 | async-start | bytes 1048576 | tf_op jit(solution)/shard_map/all_to_all | solution.py:115
  226.3 6.3 %all-to-all-done.7 = bf16[32,2,4096]{2,1,0:T(2,128)(2,1)S(1)} async-done(((bf16[32,2,4096]{2,1,0:T(2,128)(2,1)}), bf16[32,2,4096]{2,1,0:T(2,128)(2,1)S(1)}, u32[]{:S(2)}, u32[]{:S(2)}) %all-to-all-start.7) | async-done | bytes 524320 | tf_op jit(solution)/shard_map/all_to_all | solution.py:115
  232.6 8.0 %all-to-all-start.6 = ((bf16[16,2,32,256]{3,1,2,0:T(2,128)(2,1)}), bf16[16,2,32,256]{3,1,2,0:T(2,128)(2,1)S(1)}, u32[]{:S(2)}, u32[]{:S(2)}) async-start(bf16[16,2,32,256]{3,1,2,0:T(2,128)(2,1)} %constant_dynamic-update-slice_fusion), calls=%async_computation.6 | async-start | bytes 1048576 | tf_op jit(solution)/shard_map/all_to_all | solution.py:119
  241.2 1.1 copy.65
  242.2 10.2 %all-to-all-done.6 = bf16[16,2,32,256]{3,1,2,0:T(2,128)(2,1)S(1)} async-done(((bf16[16,2,32,256]{3,1,2,0:T(2,128)(2,1)}), bf16[16,2,32,256]{3,1,2,0:T(2,128)(2,1)S(1)}, u32[]{:S(2)}, u32[]{:S(2)}) %all-to-all-start.6) | async-done | bytes 524320 | tf_op jit(solution)/shard_map/all_to_all | solution.py:119
  252.5 6.9 %all-to-all-start.8 = ((bf16[32,32,256]{2,1,0:T(8,128)(2,1)}), bf16[32,32,256]{2,1,0:T(8,128)(2,1)S(1)}, u32[]{:S(2)}, u32[]{:S(2)}) async-start(bf16[32,32,256]{2,1,0:T(8,128)(2,1)} %copy.65), calls=%async_computation.8 | async-start | bytes 1048576 | tf_op jit(solution)/shard_map/all_to_all | solution.py:124
  259.3 9.4 %multiply_convert_fusion.2 = (bf16[512,1024]{0,1:T(8,128)(2,1)S(1)}, bf16[512,1024]{0,1:T(8,128)(2,1)}) fusion(f32[512]{0:T(512)S(1)} %fusion.70), kind=kLoop, calls=%fused_computation.55 | loop fusion | flops 12058624 | bytes 2099200 | tf_op jit(solution)/shard_map/convert.7
  269.7 1.4 all-to-all-done.8
  271.1 2.6 fusion.34
  273.7 2.0 copy.67
  275.8 6.8 %all-to-all-start.9 = ((bf16[2,1024,256]{2,0,1:T(2,128)(2,1)}), bf16[2,1024,256]{2,0,1:T(2,128)(2,1)}, u32[]{:S(2)}, u32[]{:S(2)}) async-start(bf16[2,1024,256]{2,0,1:T(2,128)(2,1)} %copy.67), calls=%async_computation.9 | async-start | bytes 2097152 | tf_op jit(solution)/shard_map/all_to_all | solution.py:137
  283.3 8.8 %collective-permute-start = (bf16[1,64,256]{2,1,0:T(8,128)(2,1)S(1)}, bf16[1,64,256]{2,1,0:T(8,128)(2,1)S(1)}, u32[]{:S(2)}, u32[]{:S(2)}) collective-permute-start(bf16[1,64,256]{2,1,0:T(8,128)(2,1)S(1)} %get-tuple-element.9), channel_id=1, source_target_pairs={{0,16},{16,32},{32,48},{48,64},{64,80},{80,96},{96,112},{112,128},... | collective-permute-start | bytes 98312 | tf_op jit(solution)/shard_map/ppermute | solution.py:15
  292.2 2.2 collective-permute-start.1
  294.4 4.0 %collective-permute-done = bf16[1,64,256]{2,1,0:T(8,128)(2,1)S(1)} collective-permute-done((bf16[1,64,256]{2,1,0:T(8,128)(2,1)S(1)}, bf16[1,64,256]{2,1,0:T(8,128)(2,1)S(1)}, u32[]{:S(2)}, u32[]{:S(2)}) %collective-permute-start) | collective-permute-done | bytes 32800 | tf_op jit(solution)/shard_map/ppermute | solution.py:15
  298.4 8.2 %collective-permute-done.1 = bf16[1,64,256]{2,1,0:T(8,128)(2,1)S(1)} collective-permute-done((bf16[1,64,256]{2,1,0:T(8,128)(2,1)S(1)}, bf16[1,64,256]{2,1,0:T(8,128)(2,1)S(1)}, u32[]{:S(2)}, u32[]{:S(2)}) %collective-permute-start.1) | collective-permute-done | bytes 32800 | tf_op jit(solution)/shard_map/ppermute | solution.py:16
  306.6 1.0 pad_maximum_fusion.5
  307.6 1.9 collective-permute-start.2
  309.6 3.4 %collective-permute-start.3 = (bf16[34,1,256]{2,1,0:T(2,128)(2,1)S(1)}, bf16[34,1,256]{2,1,0:T(2,128)(2,1)S(1)}, u32[]{:S(2)}, u32[]{:S(2)}) collective-permute-start(bf16[34,1,256]{2,1,0:T(2,128)(2,1)S(1)} %get-tuple-element.8), channel_id=1, source_target_pairs={{1,0},{2,1},{3,2},{4,3},{5,4},{6,5},{7,6},{8,7},{9,8},{10,9},{11,1... | collective-permute-start | bytes 52232 | tf_op jit(solution)/shard_map/ppermute | solution.py:16
  313.6 4.6 %collective-permute-done.3 = bf16[34,1,256]{2,1,0:T(2,128)(2,1)S(1)} collective-permute-done((bf16[34,1,256]{2,1,0:T(2,128)(2,1)S(1)}, bf16[34,1,256]{2,1,0:T(2,128)(2,1)S(1)}, u32[]{:S(2)}, u32[]{:S(2)}) %collective-permute-start.3) | collective-permute-done | bytes 17440 | tf_op jit(solution)/shard_map/ppermute | solution.py:16
  318.2 2.3 maximum_maximum_fusion.3
  320.5 2.1 convert_bitcast_fusion
  323.4 5.2 %fusion.14 = bf16[32,64,256]{2,1,0:T(8,128)(2,1)} fusion(bf16[32,64,256]{2,1,0:T(8,128)(2,1)S(1)} %copy-done, f32[16,2,64,256]{3,2,1,0:T(8,128)S(1)} %copy.68, bf16[32,64,256]{2,1,0:T(8,128)(2,1)} %fusion.12, bf16[34,65,256]{2,1,0:T(8,128)(2,1)S(1)} %get-tuple-element.6, bf16[1,64,256]{2,1,0:T(8,128)(2,1)S(1)} %copy-done.9, ...), kind=kLoop, calls=%fused_computation.31 | loop fusion | flops 16777216 | bytes 11609088 | tf_op jit(solution)/shard_map/convert_element_type | solution.py:138
  (97 shorter events, 25.9 us)
Async XLA Ops:
  0.0 3.6 %copy-start = (bf16[32,64,256]{2,1,0:T(8,128)(2,1)S(1)}, bf16[32,64,256]{2,1,0:T(8,128)(2,1)}, u32[]{:S(2)}) copy-start(bf16[32,64,256]{2,1,0:T(8,128)(2,1)} %param.5) | copy-start | bytes 3145732
  0.0 3.6 %copy-start.21 = (f32[256]{0:T(256)S(1)}, f32[256]{0:T(256)}, u32[]{:S(2)}) copy-start(f32[256]{0:T(256)} %param.6) | copy-start | bytes 3076
  5.1 29.4 %all-to-all-start = ((bf16[32,64,256]{2,1,0:T(8,128)(2,1)}), bf16[32,64,256]{2,1,0:T(8,128)(2,1)S(1)}, u32[]{:S(2)}, u32[]{:S(2)}) async-start(bf16[32,64,256]{2,1,0:T(8,128)(2,1)} %fusion.12), calls=%async_computation | async-start | bytes 2097152 | tf_op jit(solution)/shard_map/all_to_all | solution.py:58
  34.5 1.2 copy-start.3
  38.4 19.3 %all-to-all-start.1 = ((bf16[2,512,256]{2,0,1:T(2,128)(2,1)}), bf16[2,512,256]{2,0,1:T(2,128)(2,1)S(1)}, u32[]{:S(2)}, u32[]{:S(2)}) async-start(bf16[2,512,256]{2,0,1:T(2,128)(2,1)} %copy.49), calls=%async_computation.1 | async-start | bytes 1048576 | tf_op jit(solution)/shard_map/all_to_all | solution.py:71
  57.7 17.8 %all-to-all-start.3 = ((bf16[2,512,256]{2,0,1:T(2,128)(2,1)}), bf16[2,512,256]{2,0,1:T(2,128)(2,1)S(1)}, u32[]{:S(2)}, u32[]{:S(2)}) async-start(bf16[2,512,256]{2,0,1:T(2,128)(2,1)} %copy.53), calls=%async_computation.3 | async-start | bytes 1048576 | tf_op jit(solution)/shard_map/all_to_all | solution.py:72
  75.5 34.8 %all-to-all-start.2 = ((bf16[32,32,256]{2,0,1:T(8,128)(2,1)}), bf16[32,32,256]{2,0,1:T(8,128)(2,1)S(1)}, u32[]{:S(2)}, u32[]{:S(2)}) async-start(bf16[32,32,256]{2,0,1:T(8,128)(2,1)} %copy.52), calls=%async_computation.2 | async-start | bytes 1048576 | tf_op jit(solution)/shard_map/all_to_all | solution.py:75
  110.3 0.8 copy-start.5
  111.2 41.6 %all-to-all-start.4 = ((bf16[32,32,256]{2,0,1:T(8,128)(2,1)}), bf16[32,32,256]{2,0,1:T(8,128)(2,1)}, u32[]{:S(2)}, u32[]{:S(2)}) async-start(bf16[32,32,256]{2,0,1:T(8,128)(2,1)} %copy.56), calls=%async_computation.4 | async-start | bytes 1048576 | tf_op jit(solution)/shard_map/all_to_all | solution.py:76
  167.6 0.9 copy-start.4
  168.9 0.9 copy-start.10
  170.9 1.6 copy-start.1
  170.9 2.2 copy-start.2
  178.2 29.3 %all-to-all-start.5 = ((bf16[32,2,4096]{2,1,0:T(2,128)(2,1)}), bf16[32,2,4096]{2,1,0:T(2,128)(2,1)S(1)}, u32[]{:S(2)}, u32[]{:S(2)}) async-start(bf16[32,2,4096]{2,1,0:T(2,128)(2,1)} %reshape.164), calls=%async_computation.5 | async-start | bytes 1048576 | tf_op jit(solution)/shard_map/all_to_all | solution.py:114
  207.5 25.1 %all-to-all-start.7 = ((bf16[32,2,4096]{2,1,0:T(2,128)(2,1)}), bf16[32,2,4096]{2,1,0:T(2,128)(2,1)S(1)}, u32[]{:S(2)}, u32[]{:S(2)}) async-start(bf16[32,2,4096]{2,1,0:T(2,128)(2,1)} %reshape.162), calls=%async_computation.7 | async-start | bytes 1048576 | tf_op jit(solution)/shard_map/all_to_all | solution.py:115
  232.6 19.9 %all-to-all-start.6 = ((bf16[16,2,32,256]{3,1,2,0:T(2,128)(2,1)}), bf16[16,2,32,256]{3,1,2,0:T(2,128)(2,1)S(1)}, u32[]{:S(2)}, u32[]{:S(2)}) async-start(bf16[16,2,32,256]{3,1,2,0:T(2,128)(2,1)} %constant_dynamic-update-slice_fusion), calls=%async_computation.6 | async-start | bytes 1048576 | tf_op jit(solution)/shard_map/all_to_all | solution.py:119
  252.5 18.6 %all-to-all-start.8 = ((bf16[32,32,256]{2,1,0:T(8,128)(2,1)}), bf16[32,32,256]{2,1,0:T(8,128)(2,1)S(1)}, u32[]{:S(2)}, u32[]{:S(2)}) async-start(bf16[32,32,256]{2,1,0:T(8,128)(2,1)} %copy.65), calls=%async_computation.8 | async-start | bytes 1048576 | tf_op jit(solution)/shard_map/all_to_all | solution.py:124
  275.8 37.2 %copy-start.11 = (f32[3,3,256]{2,1,0:T(4,128)S(1)}, f32[3,3,256]{2,1,0:T(4,128)}, u32[]{:S(2)}) copy-start(f32[3,3,256]{2,1,0:T(4,128)} %param.9) | copy-start | bytes 27652
  275.8 44.7 %all-to-all-start.9 = ((bf16[2,1024,256]{2,0,1:T(2,128)(2,1)}), bf16[2,1024,256]{2,0,1:T(2,128)(2,1)}, u32[]{:S(2)}, u32[]{:S(2)}) async-start(bf16[2,1024,256]{2,0,1:T(2,128)(2,1)} %copy.67), calls=%async_computation.9 | async-start | bytes 2097152 | tf_op jit(solution)/shard_map/all_to_all | solution.py:137
  283.3 15.0 %collective-permute-start = (bf16[1,64,256]{2,1,0:T(8,128)(2,1)S(1)}, bf16[1,64,256]{2,1,0:T(8,128)(2,1)S(1)}, u32[]{:S(2)}, u32[]{:S(2)}) collective-permute-start(bf16[1,64,256]{2,1,0:T(8,128)(2,1)S(1)} %get-tuple-element.9), channel_id=1, source_target_pairs={{0,16},{16,32},{32,48},{48,64},{64,80},{80,96},{96,112},{112,128},... | collective-permute-start | bytes 98312 | tf_op jit(solution)/shard_map/ppermute | solution.py:15
  292.2 14.4 %collective-permute-start.1 = (bf16[1,64,256]{2,1,0:T(8,128)(2,1)S(1)}, bf16[1,64,256]{2,1,0:T(8,128)(2,1)S(1)}, u32[]{:S(2)}, u32[]{:S(2)}) collective-permute-start(bf16[1,64,256]{2,1,0:T(8,128)(2,1)S(1)} %get-tuple-element.10), channel_id=1, source_target_pairs={{16,0},{32,16},{48,32},{64,48},{80,64},{96,80},{112,96},{128,112},... | collective-permute-start | bytes 98312 | tf_op jit(solution)/shard_map/ppermute | solution.py:16
  298.4 19.8 %copy-start.6 = (bf16[1,64,256]{2,1,0:T(8,128)(2,1)}, bf16[1,64,256]{2,1,0:T(8,128)(2,1)S(1)}, u32[]{:S(2)}) copy-start(bf16[1,64,256]{2,1,0:T(8,128)(2,1)S(1)} %collective-permute-done) | copy-start | bytes 98308
  306.6 11.6 %copy-start.8 = (bf16[1,64,256]{2,1,0:T(8,128)(2,1)}, bf16[1,64,256]{2,1,0:T(8,128)(2,1)S(1)}, u32[]{:S(2)}) copy-start(bf16[1,64,256]{2,1,0:T(8,128)(2,1)S(1)} %collective-permute-done.1) | copy-start | bytes 98308
  307.6 5.9 %collective-permute-start.2 = (bf16[34,1,256]{2,1,0:T(2,128)(2,1)S(1)}, bf16[34,1,256]{2,1,0:T(2,128)(2,1)S(1)}, u32[]{:S(2)}, u32[]{:S(2)}) collective-permute-start(bf16[34,1,256]{2,1,0:T(2,128)(2,1)S(1)} %get-tuple-element.7), channel_id=1, source_target_pairs={{0,1},{1,2},{2,3},{3,4},{4,5},{5,6},{6,7},{7,8},{8,9},{9,10},{10,1... | collective-permute-start | bytes 52232 | tf_op jit(solution)/shard_map/ppermute | solution.py:15
  309.6 8.6 %collective-permute-start.3 = (bf16[34,1,256]{2,1,0:T(2,128)(2,1)S(1)}, bf16[34,1,256]{2,1,0:T(2,128)(2,1)S(1)}, u32[]{:S(2)}, u32[]{:S(2)}) collective-permute-start(bf16[34,1,256]{2,1,0:T(2,128)(2,1)S(1)} %get-tuple-element.8), channel_id=1, source_target_pairs={{1,0},{2,1},{3,2},{4,3},{5,4},{6,5},{7,6},{8,7},{9,8},{10,9},{11,1... | collective-permute-start | bytes 52232 | tf_op jit(solution)/shard_map/ppermute | solution.py:16
  322.6 0.8 copy-start.7
  322.6 0.8 copy-start.9
  322.6 0.8 copy-start.12
  322.6 0.8 copy-start.13
  322.6 0.7 copy-start.14
  322.6 0.7 copy-start.15
  322.7 0.7 copy-start.16
  322.7 0.7 copy-start.17
  322.7 0.7 copy-start.18
  322.7 0.7 copy-start.19
  322.7 0.7 copy-start.20
